TPU v7x, 1024 devices: a whole 4x8x16 slice. The times are simulated.
1024 devices in a mesh: dp: 8 (over x, core), ctx: 16 (over z), rep: 8 (over y).
Axes of the slice: x: 4, y: 8, z: 16, core: 2. Of those that a mesh axis runs over, the one named last changes fastest.
Arguments:
- inputs: bfloat16 [8, 16384, 4096], P('dp', ('ctx', 'rep')), may hold values from -24 to 24
- queries: bfloat16 [8, 16384, 2048], P('dp', ('ctx', 'rep')), may hold values from -24 to 24
- keys: bfloat16 [8, 16384, 512], P('dp', ('ctx', 'rep')), may hold values from -24 to 24
- values: bfloat16 [8, 16384, 512], P('dp', ('ctx', 'rep')), may hold values from -6 to 6
- grad_out: bfloat16 [8, 16384, 2048], P('dp', ('ctx', 'rep')), may hold values from -0.01953125 to 0.01953125
- doc_ids: int32 [8, 16384], P('dp', ('ctx', 'rep')), may hold values from 0 to 511, never falling along the last dimension, each value on 1 to 128 neighbouring positions
- plan: int32 [8, 512], P('dp', ('ctx', 'rep')), may hold values from 0 to 7, as said below
Outputs:
- placed_out: bfloat16 [8, 16384, 2048], P('dp', ('ctx', 'rep'))
- weight_grad: float32 [4096, 512], P('ctx')
Inputs may be any that keep to these rules, and one draw needn't show every extreme that they name: `doc_ids`: ids never fall along a micro-batch; a document holds at most 128 positions. `plan`: for one sequence shard, the 4 blocks of a micro-batch go to 4 different micro-batches (itself possibly), and every micro-batch receives exactly one block of each local block index.
All inputs are finite; a program needn't handle non-finite values.
Results may differ from a plain program's by a relative error of at most 0.017.
Values may be sent and summed in bfloat16 or wider, within the bound.
A program may use at most 32 MiB of HBM per device.

v0:
```python
import math

import jax
import jax.numpy as jnp
from jax import lax
from jax.sharding import PartitionSpec as P

HEAD_DIM = 128
KV_HEADS = 4
GROUP = 4


def from_behind(value, axis, by):
    devices = lax.axis_size(axis)
    pairs = [(i, i + by) for i in range(devices) if 0 <= i + by < devices]
    return lax.ppermute(value, axis, pairs)


def block_attention(query_rows, key_rows, query_docs, key_docs, query_pos, key_pos):
    count_q = query_rows.shape[0]
    count_k = key_rows.shape[0]
    queries4 = query_rows.reshape(count_q, KV_HEADS, GROUP, HEAD_DIM)
    keys3 = key_rows.reshape(count_k, KV_HEADS, HEAD_DIM)
    scores = jnp.einsum("tgrd,ugd->grtu", queries4, keys3, preferred_element_type=jnp.float32) * (
        1.0 / math.sqrt(HEAD_DIM)
    )
    allowed = (query_docs[:, None] == key_docs[None, :]) & (key_pos[None, :] <= query_pos[:, None])
    scores = jnp.where(allowed, scores, -jnp.inf)
    row_max = jnp.max(scores, axis=-1, keepdims=True)
    exponent = jnp.exp(scores - row_max)
    row_sum = jnp.sum(exponent, axis=-1, keepdims=True)
    probabilities = (exponent / row_sum).astype(jnp.bfloat16)
    return (probabilities, row_max, row_sum)


def local(inputs, queries, keys, values, grad_out, doc_ids, plan):
    token_count = inputs.shape[1]
    q_width = queries.shape[2]
    kv_width = keys.shape[2]
    input_rows = inputs[0]
    query_rows = queries[0]
    key_rows = keys[0]
    value_rows = values[0]
    grad_rows = grad_out[0]
    row_docs = doc_ids[0]
    shard_index = lax.axis_index(("ctx", "rep"))
    query_pos = shard_index * token_count + jnp.arange(token_count, dtype=jnp.int32)
    prior_keys, prior_values, prior_docs = from_behind(
        (key_rows, value_rows, row_docs + 1), ("ctx", "rep"), 1
    )
    keys_all = jnp.concatenate([prior_keys, key_rows], 0)
    values_all = jnp.concatenate([prior_values, value_rows], 0)
    docs_all = jnp.concatenate([prior_docs - 1, row_docs], 0)
    pos_all = jnp.concatenate([query_pos - token_count, query_pos], 0)
    probabilities, row_max, row_sum = block_attention(
        query_rows, keys_all, row_docs, docs_all, query_pos, pos_all
    )
    values3 = values_all.reshape(2 * token_count, KV_HEADS, HEAD_DIM)
    attended = jnp.einsum(
        "grtu,ugd->tgrd", probabilities, values3, preferred_element_type=jnp.float32
    ).astype(jnp.bfloat16)
    attended = attended.reshape(token_count, q_width)
    owner_count = lax.axis_size("dp")
    block_count = plan.shape[1]
    block_rows = token_count // block_count
    targets = plan[0]
    owner_index = jnp.arange(owner_count, dtype=jnp.int32)
    chosen = owner_index[:, None] == targets[None, :]
    pieces = attended.reshape(block_count, block_rows, q_width)
    outgoing = jnp.einsum(
        "pi,ibf->pbf", chosen.astype(jnp.bfloat16), pieces, preferred_element_type=jnp.float32
    ).astype(jnp.bfloat16)
    block_labels = jnp.sum(
        chosen.astype(jnp.int32) * (jnp.arange(block_count, dtype=jnp.int32)[None, :] + 1),
        axis=1,
        keepdims=True,
    )
    arrived, arrived_labels = (
        lax.all_to_all(outgoing, "dp", split_axis=0, concat_axis=0, tiled=True),
        lax.all_to_all(block_labels, "dp", split_axis=0, concat_axis=0, tiled=True),
    )
    matched = arrived_labels[:, 0][None, :] == jnp.arange(block_count, dtype=jnp.int32)[:, None] + 1
    placed = jnp.einsum(
        "ip,pbf->ibf", matched.astype(jnp.bfloat16), arrived, preferred_element_type=jnp.float32
    ).astype(jnp.bfloat16)
    placed = placed.reshape(1, token_count, q_width)
    grads4 = grad_rows.reshape(token_count, KV_HEADS, GROUP, HEAD_DIM)
    value_grad = jnp.einsum(
        "grtu,tgrd->ugd", probabilities, grads4, preferred_element_type=jnp.float32
    )
    value_grad = value_grad.reshape(2 * token_count, kv_width)
    returned = from_behind(
        value_grad[:token_count].astype(jnp.bfloat16), ("ctx", "rep"), -1
    ).astype(jnp.float32)
    grad_values = (value_grad[token_count:] + returned).astype(jnp.bfloat16)
    partial_grad = lax.psum_scatter(
        jnp.einsum("tc,tf->cf", input_rows, grad_values, preferred_element_type=jnp.float32).astype(
            jnp.bfloat16
        ),
        "ctx",
        scatter_dimension=0,
        tiled=True,
    ).astype(jnp.float32)
    weight_grad = lax.psum(partial_grad, ("dp", "rep"))
    return (placed, weight_grad)


def solution(mesh):
    in_specs = (
        P("dp", ("ctx", "rep"), None),
        P("dp", ("ctx", "rep"), None),
        P("dp", ("ctx", "rep"), None),
        P("dp", ("ctx", "rep"), None),
        P("dp", ("ctx", "rep"), None),
        P("dp", ("ctx", "rep")),
        P("dp", ("ctx", "rep")),
    )
    out_specs = (P("dp", ("ctx", "rep"), None), P("ctx", None))
    return jax.shard_map(local, mesh=mesh, in_specs=in_specs, out_specs=out_specs, check_vma=False)
```

profile of v0, /device:TPU:1, one launch (start us, length us, event | category | flops | bytes accessed | tf_op | source)
XLA Modules:
  0.0 376.9 jit_solution(7215207819716869027)
XLA Ops:
  7.2 0.7 broadcast_add_fusion.2
  8.0 4.0 %collective-permute-start.1 = (s32[128]{0:T(128)S(1)}, s32[128]{0:T(128)S(1)}, u32[]{:S(2)}, u32[]{:S(2)}) collective-permute-start(s32[128]{0:T(128)S(1)} %broadcast_add_fusion.2), channel_id=1, source_target_pairs={{0,1},{1,2},{2,3},{3,4},{4,5},{5,6},{6,7},{7,8},{8,9},{9,10},{10,1... | collective-permute-start | bytes 1544 | tf_op jit(solution)/shard_map/ppermute | solution.py:16
  12.0 1.0 copy.49
  13.0 3.2 collective-permute-start.2
  16.4 1.4 reshape_squeeze.6
  17.8 1.3 copy.68
  19.5 2.1 fusion.36
  21.6 2.1 convolution_bitcast_fusion
  23.7 1.3 collective-permute-start.3
  25.0 4.4 %collective-permute-done.3 = bf16[128,512]{0,1:T(8,128)(2,1)S(1)} collective-permute-done((bf16[128,512]{0,1:T(8,128)(2,1)S(1)}, bf16[128,512]{0,1:T(8,128)(2,1)S(1)}, u32[]{:S(2)}, u32[]{:S(2)}) %collective-permute-start.3) | collective-permute-done | bytes 131104 | tf_op jit(solution)/shard_map/ppermute | solution.py:16
  29.5 3.2 fusion.1
  32.7 0.9 copy-done.1
  33.5 4.2 %collective-permute-start = (bf16[128,512]{1,0:T(8,128)(2,1)S(1)}, bf16[128,512]{1,0:T(8,128)(2,1)S(1)}, u32[]{:S(2)}, u32[]{:S(2)}) collective-permute-start(bf16[128,512]{1,0:T(8,128)(2,1)S(1)} %bitcast.66), channel_id=1, source_target_pairs={{0,1},{1,2},{2,3},{3,4},{4,5},{5,6},{6,7},{7,8},{8,9},{9,10},{10,1... | collective-permute-start | bytes 393224 | tf_op jit(solution)/shard_map/ppermute | solution.py:16
  37.9 0.7 copy.46
  38.6 13.4 %all-to-all-start = ((s32[8,1,1]{2,1,0:T(1,128)}), s32[8,1,1]{2,1,0:T(1,128)S(1)}, u32[]{:S(2)}, u32[]{:S(2)}) async-start(s32[8,1,1]{2,1,0:T(1,128)} %copy.46), calls=%async_computation | async-start | bytes 8192 | tf_op jit(solution)/shard_map/all_to_all | solution.py:80
  52.2 1.9 fusion.3
  55.6 1.6 copy.57
  57.2 4.8 %all-to-all-start.1 = ((bf16[8,32,2048]{2,1,0:T(8,128)(2,1)}), bf16[8,32,2048]{2,1,0:T(8,128)(2,1)S(1)}, u32[]{:S(2)}, u32[]{:S(2)}) async-start(bf16[8,32,2048]{2,1,0:T(8,128)(2,1)} %copy.57), calls=%async_computation.1 | async-start | bytes 2097152 | tf_op jit(solution)/shard_map/all_to_all | solution.py:79
  62.3 14.9 %all-to-all-done.1 = bf16[8,32,2048]{2,1,0:T(8,128)(2,1)S(1)} async-done(((bf16[8,32,2048]{2,1,0:T(8,128)(2,1)}), bf16[8,32,2048]{2,1,0:T(8,128)(2,1)S(1)}, u32[]{:S(2)}, u32[]{:S(2)}) %all-to-all-start.1) | async-done | bytes 1048608 | tf_op jit(solution)/shard_map/all_to_all | solution.py:79
  77.1 0.8 convolution_convert_fusion.2
  77.9 1.1 copy.59
  79.0 37.2 %reduce-scatter.2.cloned.1.call-done = bf16[256,512]{0,1:T(8,128)(2,1)} async-done(((bf16[4096,512]{0,1:T(8,128)(2,1)}), bf16[256,512]{0,1:T(8,128)(2,1)}) %reduce-scatter.2.cloned.1.call-update) | async-done | bytes 262160 | tf_op jit(solution)/shard_map/reduce_scatter | solution.py:96
  116.2 252.8 %all-reduce.1 = f32[256,512]{0,1:T(8,128)S(1)} all-reduce(bf16[256,512]{0,1:T(8,128)(2,1)} %reduce-scatter.2.cloned.1.call-done), channel_id=1, replica_groups=mesh['dp'=8,'ctx'=16,'rep'=8] {'dp','rep'}, use_global_device_ids=true, to_apply=%region_4.5 | all-reduce | flops 131072 | bytes 786432 | tf_op jit(solution)/shard_map/psum | solution.py:104
  369.1 1.0 copy.62
  (32 shorter events, 2.6 us)
Async XLA Ops:
  7.2 22.3 %copy-start = (bf16[1,128,4096]{2,1,0:T(8,128)(2,1)S(1)}, bf16[1,128,4096]{2,1,0:T(8,128)(2,1)}, u32[]{:S(2)}) copy-start(bf16[1,128,4096]{2,1,0:T(8,128)(2,1)} %param.7) | copy-start | bytes 3145732
  7.2 12.0 %copy-start.2 = (s32[1,128]{1,0:T(1,128)S(1)}, s32[1,128]{1,0:T(1,128)}, u32[]{:S(2)}) copy-start(s32[1,128]{1,0:T(1,128)} %param.12) | copy-start | bytes 1540
  7.2 109.0 %reduce-scatter.2.cloned.1.call-start = ((), (), s32[]{:S(2)}) async-start(), calls=%async_computation.3 | async-start | bytes 4456448 | tf_op jit(solution)/shard_map/reduce_scatter | solution.py:96
  8.0 11.2 %collective-permute-start.1 = (s32[128]{0:T(128)S(1)}, s32[128]{0:T(128)S(1)}, u32[]{:S(2)}, u32[]{:S(2)}) collective-permute-start(s32[128]{0:T(128)S(1)} %broadcast_add_fusion.2), channel_id=1, source_target_pairs={{0,1},{1,2},{2,3},{3,4},{4,5},{5,6},{6,7},{7,8},{8,9},{9,10},{10,1... | collective-permute-start | bytes 1544 | tf_op jit(solution)/shard_map/ppermute | solution.py:16
  13.0 6.3 %collective-permute-start.2 = (bf16[128,512]{0,1:T(8,128)(2,1)S(1)}, bf16[128,512]{0,1:T(8,128)(2,1)S(1)}, u32[]{:S(2)}, u32[]{:S(2)}) collective-permute-start(bf16[128,512]{0,1:T(8,128)(2,1)S(1)} %bitcast.64), channel_id=1, source_target_pairs={{0,1},{1,2},{2,3},{3,4},{4,5},{5,6},{6,7},{7,8},{8,9},{9,10},{10,1... | collective-permute-start | bytes 393224 | tf_op jit(solution)/shard_map/ppermute | solution.py:16
  23.7 5.7 %collective-permute-start.3 = (bf16[128,512]{0,1:T(8,128)(2,1)S(1)}, bf16[128,512]{0,1:T(8,128)(2,1)S(1)}, u32[]{:S(2)}, u32[]{:S(2)}) collective-permute-start(bf16[128,512]{0,1:T(8,128)(2,1)S(1)} %bitcast.69), channel_id=1, source_target_pairs={{1,0},{2,1},{3,2},{4,3},{5,4},{6,5},{7,6},{8,7},{9,8},{10,9},{11,1... | collective-permute-start | bytes 393224 | tf_op jit(solution)/shard_map/ppermute | solution.py:16
  32.6 0.9 copy-start.1
  32.6 5.2 %copy-start.3 = (s32[1,4]{1,0:T(1,128)S(1)}, s32[1,4]{1,0:T(1,128)}, u32[]{:S(2)}) copy-start(s32[1,4]{1,0:T(1,128)} %param.13) | copy-start | bytes 52
  33.5 18.5 %collective-permute-start = (bf16[128,512]{1,0:T(8,128)(2,1)S(1)}, bf16[128,512]{1,0:T(8,128)(2,1)S(1)}, u32[]{:S(2)}, u32[]{:S(2)}) collective-permute-start(bf16[128,512]{1,0:T(8,128)(2,1)S(1)} %bitcast.66), channel_id=1, source_target_pairs={{0,1},{1,2},{2,3},{3,4},{4,5},{5,6},{6,7},{7,8},{8,9},{9,10},{10,1... | collective-permute-start | bytes 393224 | tf_op jit(solution)/shard_map/ppermute | solution.py:16
  38.6 18.6 %all-to-all-start = ((s32[8,1,1]{2,1,0:T(1,128)}), s32[8,1,1]{2,1,0:T(1,128)S(1)}, u32[]{:S(2)}, u32[]{:S(2)}) async-start(s32[8,1,1]{2,1,0:T(1,128)} %copy.46), calls=%async_computation | async-start | bytes 8192 | tf_op jit(solution)/shard_map/all_to_all | solution.py:80
  57.2 19.9 %all-to-all-start.1 = ((bf16[8,32,2048]{2,1,0:T(8,128)(2,1)}), bf16[8,32,2048]{2,1,0:T(8,128)(2,1)S(1)}, u32[]{:S(2)}, u32[]{:S(2)}) async-start(bf16[8,32,2048]{2,1,0:T(8,128)(2,1)} %copy.57), calls=%async_computation.1 | async-start | bytes 2097152 | tf_op jit(solution)/shard_map/all_to_all | solution.py:79
Sparse Core Ops, SparseCore 0:
  32.8 83.3 reduce-scatter.1
where the time goes:
time: 383 us; the launch traced here: 377 us
  blocking collectives  253 us (66%)
  waiting for transfers between devices  56.5 us (15%)
  starting transfers between devices  31 us (8%)
  between operations  14.3 us (4%)
  matrix products  10.8 us (3%)
  local copies, waits for them, and re-layouts  10.3 us (3%)
    psum x1, blocking collectives, local(): weight_grad = lax.psum(partial_grad, ('dp', 'rep'))  253 us
    reduce_scatter x1, waiting for transfers between devices, local(): lax.psum_scatter(jnp.einsum('tc,tf->cf', input_rows, grad_values, preferr...  37.2 us
    all_to_all x1, waiting for transfers between devices, local(): lax.all_to_all(outgoing, 'dp', split_axis=0, concat_axis=0, tiled=True)  14.9 us
    all_to_all x1, starting transfers between devices, local(): lax.all_to_all(block_labels, 'dp', split_axis=0, concat_axis=0, tiled=True)  13.4 us
    ppermute x4, starting transfers between devices, from_behind(): return lax.ppermute(value, axis, pairs)  12.8 us
  transfers between devices with their start and end apart: 7, of which 3 were waited for; matrix products, arithmetic and copies ran while one was open for 3% of the time, Pallas kernels for 0%

commit v1 on v0

--- a/solution.py
+++ b/solution.py
@@ -33,6 +33,31 @@
     return (probabilities, row_max, row_sum)
 
 
+def spread_inputs(input_rows):
+    count_t, width = input_rows.shape
+    ctx, dp = lax.axis_size("ctx"), lax.axis_size("dp")
+    parts = input_rows.reshape(count_t, ctx, dp, width // (ctx * dp))
+    parts = jnp.transpose(parts, (2, 0, 1, 3)).reshape(dp, count_t, width // dp)
+    spread = lax.all_to_all(parts, "dp", split_axis=0, concat_axis=0, tiled=True)
+    return spread.reshape(dp * count_t, width // dp)
+
+
+def reduced_grad(spread_rows, grad_values):
+    ctx, dp, rep = lax.axis_size("ctx"), lax.axis_size("dp"), lax.axis_size("rep")
+    width = grad_values.shape[1]
+    all_values = lax.all_gather(grad_values, "dp", axis=0, tiled=True)
+    part = jnp.einsum("tc,tf->cf", spread_rows, all_values, preferred_element_type=jnp.float32)
+    rows = part.shape[0] // (ctx * rep)
+    part = part.astype(jnp.bfloat16).reshape(ctx, rep, rows, width)
+    part = jnp.transpose(part, (1, 0, 2, 3)).reshape(rep, ctx * rows, width)
+    part = lax.all_to_all(part, "rep", split_axis=0, concat_axis=0, tiled=True)
+    part = jnp.sum(part.astype(jnp.float32), axis=0).astype(jnp.bfloat16)
+    part = part.reshape(ctx, rows, width)
+    part = lax.all_to_all(part, "ctx", split_axis=0, concat_axis=0, tiled=True)
+    total = jnp.sum(part.astype(jnp.float32), axis=0)
+    return lax.all_gather(total, ("dp", "rep"), axis=0, tiled=True)
+
+
 def local(inputs, queries, keys, values, grad_out, doc_ids, plan):
     token_count = inputs.shape[1]
     q_width = queries.shape[2]
@@ -43,6 +68,7 @@
     value_rows = values[0]
     grad_rows = grad_out[0]
     row_docs = doc_ids[0]
+    spread_rows = spread_inputs(input_rows)
     shard_index = lax.axis_index(("ctx", "rep"))
     query_pos = shard_index * token_count + jnp.arange(token_count, dtype=jnp.int32)
     prior_keys, prior_values, prior_docs = from_behind(
@@ -93,15 +119,7 @@
         value_grad[:token_count].astype(jnp.bfloat16), ("ctx", "rep"), -1
     ).astype(jnp.float32)
     grad_values = (value_grad[token_count:] + returned).astype(jnp.bfloat16)
-    partial_grad = lax.psum_scatter(
-        jnp.einsum("tc,tf->cf", input_rows, grad_values, preferred_element_type=jnp.float32).astype(
-            jnp.bfloat16
-        ),
-        "ctx",
-        scatter_dimension=0,
-        tiled=True,
-    ).astype(jnp.float32)
-    weight_grad = lax.psum(partial_grad, ("dp", "rep"))
+    weight_grad = reduced_grad(spread_rows, grad_values)
     return (placed, weight_grad)
 
 

time: 383 us -> 208 us (0.54); the launches traced: 377 us -> 208 us
  blocking collectives: 253 us -> 53 us
  starting transfers between devices: 31 us -> 53.9 us
  waiting for transfers between devices: 56.5 us -> 61.4 us
    psum x1 -> x0, blocking collectives: 253 us -> none  [local(): weight_grad = lax.psum(partial_grad, ('dp', 'rep'))]
    all_gather x0 -> x1, blocking collectives: none -> 53 us  [reduced_grad(): return lax.all_gather(total, ('dp', 'rep'), axis=0, tiled=True)]
    reduce_scatter x1 -> x0, waiting for transfers between devices: 37.2 us -> none  [local(): lax.psum_scatter(jnp.einsum('tc,tf->cf', input_rows, grad_values, preferr...]
    all_to_all x0 -> x3, starting transfers between devices: none -> 32.1 us  [the longest x1 14.1 us: spread_inputs(): lax.all_to_all(parts, 'dp', split_axis=0, concat_axis=0, tiled=True)]
    all_to_all x0 -> x3, waiting for transfers between devices: none -> 24 us  [the longest x1 14.3 us: spread_inputs(): lax.all_to_all(parts, 'dp', split_axis=0, concat_axis=0, tiled=True)]
    ppermute x4, waiting for transfers between devices: 4.39 us -> 14.1 us  [from_behind(): return lax.ppermute(value, axis, pairs)]
    all_to_all x1, starting transfers between devices: 13.4 us -> 4.09 us  [local(): lax.all_to_all(block_labels, 'dp', split_axis=0, concat_axis=0, tiled=True)]
    all_gather x0 -> x1, waiting for transfers between devices: none -> 9.04 us  [reduced_grad(): all_values = lax.all_gather(grad_values, 'dp', axis=0, tiled=True)]
  transfers between devices with their start and end apart: 7 -> 10, of which waited for: 3 -> 6; matrix products, arithmetic and copies ran while one was open for 3% -> 9% of each run, Pallas kernels for 0% -> 0%
where the time goes in v1:
time: 208 us
  waiting for transfers between devices  61.4 us (30%)
  starting transfers between devices  53.9 us (26%)
  blocking collectives  53 us (25%)
  between operations  14.3 us (7%)
  local copies, waits for them, and re-layouts  13.5 us (6%)
  matrix products  9.59 us (5%)
    all_gather x1, blocking collectives, reduced_grad(): return lax.all_gather(total, ('dp', 'rep'), axis=0, tiled=True)  53 us
    all_to_all x1, waiting for transfers between devices, spread_inputs(): lax.all_to_all(parts, 'dp', split_axis=0, concat_axis=0, tiled=True)  14.3 us
    ppermute x4, waiting for transfers between devices, from_behind(): return lax.ppermute(value, axis, pairs)  14.1 us
    all_to_all x1, waiting for transfers between devices, local(): lax.all_to_all(outgoing, 'dp', split_axis=0, concat_axis=0, tiled=True)  14.1 us
    all_to_all x1, starting transfers between devices, spread_inputs(): lax.all_to_all(parts, 'dp', split_axis=0, concat_axis=0, tiled=True)  14.1 us
    ppermute x4, starting transfers between devices, from_behind(): return lax.ppermute(value, axis, pairs)  12 us
    all_to_all x1, starting transfers between devices, reduced_grad(): part = lax.all_to_all(part, 'ctx', split_axis=0, concat_axis=0, tiled=True)  11.6 us
    all_to_all x1, waiting for transfers between devices, reduced_grad(): part = lax.all_to_all(part, 'ctx', split_axis=0, concat_axis=0, tiled=True)  9.67 us
  transfers between devices with their start and end apart: 10, of which 6 were waited for; matrix products, arithmetic and copies ran while one was open for 9% of the time, Pallas kernels for 0%

profile of v1, /device:TPU:1, one launch (start us, length us, event | category | flops | bytes accessed | tf_op | source)
XLA Modules:
  0.0 207.6 jit_solution(16827980624217582009)
XLA Ops:
  7.9 4.0 %collective-permute-start.1 = (s32[128]{0:T(128)S(1)}, s32[128]{0:T(128)S(1)}, u32[]{:S(2)}, u32[]{:S(2)}) collective-permute-start(s32[128]{0:T(128)S(1)} %broadcast_add_fusion.2), channel_id=1, source_target_pairs={{0,1},{1,2},{2,3},{3,4},{4,5},{5,6},{6,7},{7,8},{8,9},{9,10},{10,1... | collective-permute-start | bytes 1544 | tf_op jit(solution)/shard_map/ppermute | solution.py:16
  13.0 3.2 %collective-permute-start.2 = (bf16[128,512]{0,1:T(8,128)(2,1)S(1)}, bf16[128,512]{0,1:T(8,128)(2,1)S(1)}, u32[]{:S(2)}, u32[]{:S(2)}) collective-permute-start(bf16[128,512]{0,1:T(8,128)(2,1)S(1)} %bitcast.74), channel_id=1, source_target_pairs={{0,1},{1,2},{2,3},{3,4},{4,5},{5,6},{6,7},{7,8},{8,9},{9,10},{10,1... | collective-permute-start | bytes 393224 | tf_op jit(solution)/shard_map/ppermute | solution.py:16
  16.2 1.4 reshape_squeeze.9
  17.8 1.3 copy.181
  19.4 2.1 %fusion.35 = (f32[4,4,128]{2,1,0:T(4,128)S(1)}, f32[4,4,128,256]{2,3,1,0:T(8,128)}) fusion(pred[128,256]{0,1:T(8,128)(4,1)S(1)} %compare_and_fusion, bf16[128,4,4,128]{3,2,1,0:T(4,128)(2,1)S(1)} %reshape_squeeze.9, bf16[128,4,128]{2,0,1:T(8,128)(2,1)S(1)} %copy.160, bf16[128,4,128]{2,0,1:T(8,128)(2,1)S(1)} %copy.159), kind=kOutput, calls=%fused_computation.50 | convolution fusion | flops 136839424 | bytes 2924544 | tf_op jit(solution)/shard_map/sub | solution.py:30
  21.5 2.1 convolution_bitcast_fusion
  23.6 1.4 collective-permute-start.3
  25.1 4.4 %collective-permute-done.3 = bf16[128,512]{0,1:T(8,128)(2,1)S(1)} collective-permute-done((bf16[128,512]{0,1:T(8,128)(2,1)S(1)}, bf16[128,512]{0,1:T(8,128)(2,1)S(1)}, u32[]{:S(2)}, u32[]{:S(2)}) %collective-permute-start.3) | collective-permute-done | bytes 131104 | tf_op jit(solution)/shard_map/ppermute | solution.py:16
  32.0 14.1 %all-to-all-start.2 = ((bf16[8,128,512]{1,2,0:T(8,128)(2,1)}), bf16[8,128,512]{1,2,0:T(8,128)(2,1)S(1)}, u32[]{:S(2)}, u32[]{:S(2)}) async-start(bf16[8,128,512]{1,2,0:T(8,128)(2,1)} %bitcast.27), calls=%async_computation.2 | async-start | bytes 2097152 | tf_op jit(solution)/shard_map/all_to_all | solution.py:41
  46.8 14.3 %all-to-all-done.2 = bf16[8,128,512]{1,2,0:T(8,128)(2,1)S(1)} async-done(((bf16[8,128,512]{1,2,0:T(8,128)(2,1)}), bf16[8,128,512]{1,2,0:T(8,128)(2,1)S(1)}, u32[]{:S(2)}, u32[]{:S(2)}) %all-to-all-start.2) | async-done | bytes 1048608 | tf_op jit(solution)/shard_map/all_to_all | solution.py:41
  61.2 4.1 %all-to-all-start = ((s32[8,1,1]{2,1,0:T(1,128)}), s32[8,1,1]{2,1,0:T(1,128)S(1)}, u32[]{:S(2)}, u32[]{:S(2)}) async-start(s32[8,1,1]{2,1,0:T(1,128)} %copy.154), calls=%async_computation | async-start | bytes 8192 | tf_op jit(solution)/shard_map/all_to_all | solution.py:106
  65.8 9.0 %all-gather.3.cloned.1.call-done = bf16[1024,512]{0,1:T(8,128)(2,1)} async-done(((bf16[128,512]{0,1:T(8,128)(2,1)}), bf16[1024,512]{0,1:T(8,128)(2,1)}) %all-gather.3.cloned.1.call-update) | async-done | bytes 1048592 | tf_op jit(solution)/shard_map/all_gather | solution.py:48
  74.9 2.0 fusion.2
  78.1 6.4 %all-to-all-start.3 = ((bf16[8,64,512]{2,1,0:T(8,128)(2,1)}), bf16[8,64,512]{2,1,0:T(8,128)(2,1)S(1)}, u32[]{:S(2)}, u32[]{:S(2)}) async-start(bf16[8,64,512]{2,1,0:T(8,128)(2,1)} %copy.174), calls=%async_computation.3 | async-start | bytes 1048576 | tf_op jit(solution)/shard_map/all_to_all | solution.py:53
  84.5 3.4 %collective-permute-start = (bf16[128,512]{1,0:T(8,128)(2,1)S(1)}, bf16[128,512]{1,0:T(8,128)(2,1)S(1)}, u32[]{:S(2)}, u32[]{:S(2)}) collective-permute-start(bf16[128,512]{1,0:T(8,128)(2,1)S(1)} %bitcast.76), channel_id=1, source_target_pairs={{0,1},{1,2},{2,3},{3,4},{4,5},{5,6},{6,7},{7,8},{8,9},{9,10},{10,1... | collective-permute-start | bytes 393224 | tf_op jit(solution)/shard_map/ppermute | solution.py:16
  88.0 9.8 %collective-permute-done = bf16[128,512]{1,0:T(8,128)(2,1)S(1)} collective-permute-done((bf16[128,512]{1,0:T(8,128)(2,1)S(1)}, bf16[128,512]{1,0:T(8,128)(2,1)S(1)}, u32[]{:S(2)}, u32[]{:S(2)}) %collective-permute-start) | collective-permute-done | bytes 131104 | tf_op jit(solution)/shard_map/ppermute | solution.py:16
  97.8 1.9 fusion.3
  101.3 1.5 copy.165
  102.8 5.7 %all-to-all-start.1 = ((bf16[8,32,2048]{2,1,0:T(8,128)(2,1)}), bf16[8,32,2048]{2,1,0:T(8,128)(2,1)S(1)}, u32[]{:S(2)}, u32[]{:S(2)}) async-start(bf16[8,32,2048]{2,1,0:T(8,128)(2,1)} %copy.165), calls=%async_computation.1 | async-start | bytes 2097152 | tf_op jit(solution)/shard_map/all_to_all | solution.py:105
  109.5 14.1 %all-to-all-done.1 = bf16[8,32,2048]{2,1,0:T(8,128)(2,1)S(1)} async-done(((bf16[8,32,2048]{2,1,0:T(8,128)(2,1)}), bf16[8,32,2048]{2,1,0:T(8,128)(2,1)S(1)}, u32[]{:S(2)}, u32[]{:S(2)}) %all-to-all-start.1) | async-done | bytes 1048608 | tf_op jit(solution)/shard_map/all_to_all | solution.py:105
  123.6 11.6 %all-to-all-start.4 = ((bf16[16,4,512]{2,1,0:T(4,128)(2,1)}), bf16[16,4,512]{2,1,0:T(4,128)(2,1)S(1)}, u32[]{:S(2)}, u32[]{:S(2)}) async-start(bf16[16,4,512]{2,1,0:T(4,128)(2,1)} %reshape.63), calls=%async_computation.4 | async-start | bytes 131072 | tf_op jit(solution)/shard_map/all_to_all | solution.py:56
  136.1 1.1 copy.167
  137.1 9.7 %all-to-all-done.4 = bf16[16,4,512]{2,1,0:T(4,128)(2,1)S(1)} async-done(((bf16[16,4,512]{2,1,0:T(4,128)(2,1)}), bf16[16,4,512]{2,1,0:T(4,128)(2,1)S(1)}, u32[]{:S(2)}, u32[]{:S(2)}) %all-to-all-start.4) | async-done | bytes 65568 | tf_op jit(solution)/shard_map/all_to_all | solution.py:56
  146.9 53.0 %all-gather = f32[64,4,512]{2,1,0:T(4,128)S(1)} all-gather(f32[1,4,512]{2,1,0:T(4,128)S(1)} %bitcast.81), channel_id=1, replica_groups=mesh['dp'=8,'ctx'=16,'rep'=8] {'dp','rep'}, dimensions={0}, use_global_device_ids=true | all-gather | bytes 532480 | tf_op jit(solution)/shard_map/all_gather | solution.py:58
  (47 shorter events, 11.7 us)
Async XLA Ops:
  7.2 11.9 %copy-start.2 = (s32[1,128]{1,0:T(1,128)S(1)}, s32[1,128]{1,0:T(1,128)}, u32[]{:S(2)}) copy-start(s32[1,128]{1,0:T(1,128)} %param.12) | copy-start | bytes 1540
  7.2 67.7 %all-gather.3.cloned.1.call-start = ((), (), s32[]{:S(2)}) async-start(), calls=%async_computation.5 | async-start | bytes 1179648 | tf_op jit(solution)/shard_map/all_gather | solution.py:48
  7.9 11.2 %collective-permute-start.1 = (s32[128]{0:T(128)S(1)}, s32[128]{0:T(128)S(1)}, u32[]{:S(2)}, u32[]{:S(2)}) collective-permute-start(s32[128]{0:T(128)S(1)} %broadcast_add_fusion.2), channel_id=1, source_target_pairs={{0,1},{1,2},{2,3},{3,4},{4,5},{5,6},{6,7},{7,8},{8,9},{9,10},{10,1... | collective-permute-start | bytes 1544 | tf_op jit(solution)/shard_map/ppermute | solution.py:16
  13.0 6.3 %collective-permute-start.2 = (bf16[128,512]{0,1:T(8,128)(2,1)S(1)}, bf16[128,512]{0,1:T(8,128)(2,1)S(1)}, u32[]{:S(2)}, u32[]{:S(2)}) collective-permute-start(bf16[128,512]{0,1:T(8,128)(2,1)S(1)} %bitcast.74), channel_id=1, source_target_pairs={{0,1},{1,2},{2,3},{3,4},{4,5},{5,6},{6,7},{7,8},{8,9},{9,10},{10,1... | collective-permute-start | bytes 393224 | tf_op jit(solution)/shard_map/ppermute | solution.py:16
  23.6 6.6 %copy-start = (bf16[1,128,4096]{2,1,0:T(8,128)(2,1)S(1)}, bf16[1,128,4096]{2,1,0:T(8,128)(2,1)}, u32[]{:S(2)}) copy-start(bf16[1,128,4096]{2,1,0:T(8,128)(2,1)} %param.7) | copy-start | bytes 3145732
  23.6 5.8 %collective-permute-start.3 = (bf16[128,512]{0,1:T(8,128)(2,1)S(1)}, bf16[128,512]{0,1:T(8,128)(2,1)S(1)}, u32[]{:S(2)}, u32[]{:S(2)}) collective-permute-start(bf16[128,512]{0,1:T(8,128)(2,1)S(1)} %bitcast.79), channel_id=1, source_target_pairs={{1,0},{2,1},{3,2},{4,3},{5,4},{6,5},{7,6},{8,7},{9,8},{10,9},{11,1... | collective-permute-start | bytes 393224 | tf_op jit(solution)/shard_map/ppermute | solution.py:16
  30.9 15.2 %copy-start.3 = (s32[1,4]{1,0:T(1,128)S(1)}, s32[1,4]{1,0:T(1,128)}, u32[]{:S(2)}) copy-start(s32[1,4]{1,0:T(1,128)} %param.13) | copy-start | bytes 52
  32.0 29.2 %all-to-all-start.2 = ((bf16[8,128,512]{1,2,0:T(8,128)(2,1)}), bf16[8,128,512]{1,2,0:T(8,128)(2,1)S(1)}, u32[]{:S(2)}, u32[]{:S(2)}) async-start(bf16[8,128,512]{1,2,0:T(8,128)(2,1)} %bitcast.27), calls=%async_computation.2 | async-start | bytes 2097152 | tf_op jit(solution)/shard_map/all_to_all | solution.py:41
  61.2 16.9 %all-to-all-start = ((s32[8,1,1]{2,1,0:T(1,128)}), s32[8,1,1]{2,1,0:T(1,128)S(1)}, u32[]{:S(2)}, u32[]{:S(2)}) async-start(s32[8,1,1]{2,1,0:T(1,128)} %copy.154), calls=%async_computation | async-start | bytes 8192 | tf_op jit(solution)/shard_map/all_to_all | solution.py:106
  76.9 7.6 %copy-start.1 = (bf16[1,128,512]{2,1,0:T(8,128)(2,1)S(1)}, bf16[1,128,512]{2,1,0:T(8,128)(2,1)}, u32[]{:S(2)}) copy-start(bf16[1,128,512]{2,1,0:T(8,128)(2,1)} %param.10) | copy-start | bytes 393220
  78.1 24.8 %all-to-all-start.3 = ((bf16[8,64,512]{2,1,0:T(8,128)(2,1)}), bf16[8,64,512]{2,1,0:T(8,128)(2,1)S(1)}, u32[]{:S(2)}, u32[]{:S(2)}) async-start(bf16[8,64,512]{2,1,0:T(8,128)(2,1)} %copy.174), calls=%async_computation.3 | async-start | bytes 1048576 | tf_op jit(solution)/shard_map/all_to_all | solution.py:53
  84.5 13.2 %collective-permute-start = (bf16[128,512]{1,0:T(8,128)(2,1)S(1)}, bf16[128,512]{1,0:T(8,128)(2,1)S(1)}, u32[]{:S(2)}, u32[]{:S(2)}) collective-permute-start(bf16[128,512]{1,0:T(8,128)(2,1)S(1)} %bitcast.76), channel_id=1, source_target_pairs={{0,1},{1,2},{2,3},{3,4},{4,5},{5,6},{6,7},{7,8},{8,9},{9,10},{10,1... | collective-permute-start | bytes 393224 | tf_op jit(solution)/shard_map/ppermute | solution.py:16
  102.8 20.8 %all-to-all-start.1 = ((bf16[8,32,2048]{2,1,0:T(8,128)(2,1)}), bf16[8,32,2048]{2,1,0:T(8,128)(2,1)S(1)}, u32[]{:S(2)}, u32[]{:S(2)}) async-start(bf16[8,32,2048]{2,1,0:T(8,128)(2,1)} %copy.165), calls=%async_computation.1 | async-start | bytes 2097152 | tf_op jit(solution)/shard_map/all_to_all | solution.py:105
  123.6 23.2 %all-to-all-start.4 = ((bf16[16,4,512]{2,1,0:T(4,128)(2,1)}), bf16[16,4,512]{2,1,0:T(4,128)(2,1)S(1)}, u32[]{:S(2)}, u32[]{:S(2)}) async-start(bf16[16,4,512]{2,1,0:T(4,128)(2,1)} %reshape.63), calls=%async_computation.4 | async-start | bytes 131072 | tf_op jit(solution)/shard_map/all_to_all | solution.py:56
Sparse Core Ops, SparseCore 0:
  30.3 44.4 all-gather.2

commit v2 on v0

v2 whole, which is shorter than its diff:
```python
import math

import jax
import jax.numpy as jnp
from jax import lax
from jax.experimental import pallas as pl
from jax.experimental.pallas import tpu as pltpu
from jax.sharding import PartitionSpec as P

HEAD_DIM = 128
KV_HEADS = 4
GROUP = 4
LANES = 128
MESH = pl.DeviceIdType.MESH


def kernel(
    sizes,
    x_ref, q_ref, k_ref, v_ref, g_ref, docs_ref, plan_ref,
    placed_ref, wg_ref,
    perm, xs, xg, kprev, vprev, docprev, probs, dvp, dvo, dvr, gvg, att, slots, arr,
    planrow, planall, ysend, yown, yrecv, zf, zsend, zrecv, full,
    nb_s, nb_r, x_s, x_r, gv_s, gv_r, gf_s, gf_r, a_s, a_r, p_s, p_r,
    y_s, y_r, z_s, z_r, ay_s, ay_r, ad_s, ad_r,
):
    DP, C, R = sizes
    X = DP // 2
    T, D = x_ref.shape
    W = k_ref.shape[1]
    blocks = plan_ref.shape[1]
    brow = T // blocks
    U = D // (DP * C)
    JJ = U // R
    CC = LANES // U
    NB = C // CC
    CH = CC * JJ
    f32, bf16 = jnp.float32, jnp.bfloat16

    dp, ctx, rep = lax.axis_index("dp"), lax.axis_index("ctx"), lax.axis_index("rep")
    chip, core = dp // 2, dp % 2
    shard = ctx * R + rep
    after, before = (shard + 1) % (C * R), (shard + C * R - 1) % (C * R)
    next_dev = {"ctx": after // R, "rep": after % R}
    prev_dev = {"ctx": before // R, "rep": before % R}

    def dp_to(c, k):
        return ((chip + k) % X) * 2 + (core + c) % 2

    dp_peers = [(c, k) for c in range(2) for k in range(X) if (c, k) != (0, 0)]

    barrier = pltpu.get_barrier_semaphore()

    def greet(device):
        pl.semaphore_signal(barrier, inc=1, device_id=device, device_id_type=MESH)

    greet(next_dev)
    greet(prev_dev)
    for c, k in dp_peers:
        greet({"dp": dp_to(c, k)})
    for j in range(1, R):
        greet({"rep": (rep + j) % R})
    for j in range(1, C):
        greet({"ctx": (ctx + j) % C})

    def send(src, dst, ssem, rsem, device):
        copy = pltpu.make_async_remote_copy(
            src_ref=src, dst_ref=dst, send_sem=ssem, recv_sem=rsem, device_id=device, device_id_type=MESH
        )
        copy.start()
        return copy

    lane = lax.broadcasted_iota(jnp.int32, (1, LANES), 1)
    row = jnp.zeros((1, LANES), jnp.int32)
    for i in range(blocks):
        row = jnp.where(lane == i, plan_ref[0, i], row)
    planrow[...] = row

    width = CC * DP * U
    for d in range(DP):
        o = lax.broadcasted_iota(jnp.int32, (LANES, 1), 0)
        rr, cc, jj = o // CH, (o % CH) // JJ, o % JJ
        source = cc * (DP * U) + d * U + rr * JJ + jj
        column = lax.broadcasted_iota(jnp.int32, (LANES, width), 1)
        perm[d] = jnp.where(column == source, 1.0, 0.0).astype(bf16)

    pl.semaphore_wait(barrier, 2 + (DP - 1) + (R - 1) + (C - 1))

    pending = []
    near = [
        send(k_ref, kprev, nb_s.at[0], nb_r.at[0], next_dev),
        send(v_ref, vprev, nb_s.at[1], nb_r.at[1], next_dev),
        send(docs_ref, docprev, nb_s.at[2], nb_r.at[2], next_dev),
    ]

    for b in range(NB):
        for d in range(DP):
            xs[d, b * LANES:(b + 1) * LANES, :] = lax.dot_general(
                perm[d], x_ref[:, b * width:(b + 1) * width], (((1,), (1,)), ((), ())),
                preferred_element_type=f32,
            ).astype(bf16)
    x_copies, p_copies = {}, {}
    for c, k in dp_peers:
        to = {"dp": dp_to(c, k)}
        p_copies[c, k] = send(planrow, planall.at[c, k], p_s.at[c, k], p_r.at[c, k], to)
        x_copies[c, k] = send(xs.at[dp_to(c, k)], xg.at[c, k], x_s.at[c, k], x_r.at[c, k], to)
    xg[0, 0] = xs[dp]

    docs = docs_ref[...].astype(f32)
    by_row = jnp.broadcast_to(docs, (T, T)).T
    u_pos = lax.broadcasted_iota(jnp.int32, (T, T), 1)
    t_pos = lax.broadcasted_iota(jnp.int32, (T, T), 0)
    own = jnp.where((by_row == docs) & (u_pos <= t_pos), 1.0, 0.0)
    for copy in near:
        copy.wait()
    prior = jnp.where(by_row == docprev[...].astype(f32), 1.0, 0.0) * jnp.where(shard > 0, 1.0, 0.0)
    allowed = jnp.concatenate([prior, own], axis=1)
    allowed = jnp.concatenate([allowed] * GROUP, axis=0) > 0.5

    def heads(ref, g):
        return jnp.concatenate(
            [ref[:, (g * GROUP + h) * HEAD_DIM:(g * GROUP + h + 1) * HEAD_DIM] for h in range(GROUP)], axis=0
        )

    for g in range(KV_HEADS):
        cols = slice(g * HEAD_DIM, (g + 1) * HEAD_DIM)
        keys = jnp.concatenate([kprev[:, cols], k_ref[:, cols]], axis=0)
        scores = lax.dot_general(
            heads(q_ref, g), keys, (((1,), (1,)), ((), ())), preferred_element_type=f32
        ) * (1.0 / math.sqrt(HEAD_DIM))
        scores = jnp.where(allowed, scores, -jnp.inf)
        exponent = jnp.exp(scores - jnp.max(scores, axis=-1, keepdims=True))
        p = (exponent * (1.0 / jnp.sum(exponent, axis=-1, keepdims=True))).astype(bf16)
        probs[g] = p
        dv = lax.dot_general(p, heads(g_ref, g), (((0,), (0,)), ((), ())), preferred_element_type=f32)
        dvp[:, cols] = dv[:T].astype(bf16)
        dvo[:, cols] = dv[T:]
    dv_copy = send(dvp, dvr, nb_s.at[3], nb_r.at[3], prev_dev)

    for g in range(KV_HEADS):
        cols = slice(g * HEAD_DIM, (g + 1) * HEAD_DIM)
        vals = jnp.concatenate([vprev[:, cols], v_ref[:, cols]], axis=0)
        out = jnp.dot(probs[g], vals, preferred_element_type=f32).astype(bf16)
        for h in range(GROUP):
            att[:, (g * GROUP + h) * HEAD_DIM:(g * GROUP + h + 1) * HEAD_DIM] = out[h * T:(h + 1) * T]

    dv_copy.wait()
    gvg[0, 0] = (dvo[...] + dvr[...].astype(f32)).astype(bf16)
    gv_copies = {}
    for c, k in [(1, 0)] + [(0, k) for k in range(1, X)]:
        gv_copies[c, k] = send(gvg.at[0, 0], gvg.at[c, k], gv_s.at[c, k], gv_r.at[c, k], {"dp": dp_to(c, k)})

    for p in range(DP):
        slot = jnp.zeros((brow, att.shape[1]), bf16)
        for i in range(blocks):
            weight = jnp.where(plan_ref[0, i] == p, 1.0, 0.0).astype(f32)
            slot = slot + att[i * brow:(i + 1) * brow, :] * jnp.full((1, 1), weight, f32).astype(bf16)
        slots[p] = slot
    a_copies = {}
    for c, k in dp_peers:
        a_copies[c, k] = send(
            slots.at[dp_to(c, k)], arr.at[c, k], a_s.at[c, k], a_r.at[c, k], {"dp": dp_to(c, k)}
        )

    for k in range(1, X):
        gv_copies[0, k].wait_recv()
        gv_copies[1, k] = send(gvg.at[0, k], gvg.at[1, k], gf_s.at[k], gf_r.at[k], {"dp": dp_to(1, 0)})
    for c, k in dp_peers:
        x_copies[c, k].wait_recv()
    gv_copies[1, 0].wait_recv()
    for k in range(1, X):
        gv_copies[1, k].wait_recv()

    for b in range(NB):
        rows = slice(b * LANES, (b + 1) * LANES)
        part = jnp.zeros((LANES, W), f32)
        for c in range(2):
            for k in range(X):
                part = part + jnp.dot(xg[c, k, rows, :], gvg[c, k], preferred_element_type=f32)
        yown[b] = part
        for r in range(R):
            ysend[r, b * CH:(b + 1) * CH, :] = part[r * CH:(r + 1) * CH].astype(bf16)
    y_copies = [
        send(ysend.at[(rep + j) % R], yrecv.at[j], y_s.at[j], y_r.at[j], {"rep": (rep + j) % R})
        for j in range(1, R)
    ]
    for copy in y_copies:
        copy.wait_recv()
    for b in range(NB):
        total = yown[b, pl.ds(pl.multiple_of(rep * CH, CH), CH), :]
        for j in range(1, R):
            total = total + yrecv[j, b * CH:(b + 1) * CH, :].astype(f32)
        for cc in range(CC):
            for w in range(W // LANES):
                zf[b * CC + cc, w * JJ:(w + 1) * JJ, :] = total[
                    cc * JJ:(cc + 1) * JJ, w * LANES:(w + 1) * LANES
                ]
    zsend[...] = zf[...].astype(bf16)
    z_copies = [
        send(zsend.at[(ctx + j) % C], zrecv.at[j], z_s.at[j], z_r.at[j], {"ctx": (ctx + j) % C})
        for j in range(1, C)
    ]

    for c, k in dp_peers:
        p_copies[c, k].wait_recv()
        a_copies[c, k].wait_recv()
    arr[0, 0] = slots[dp]
    planall[0, 0] = planrow[...]
    for i in range(blocks):
        result = jnp.zeros((brow, att.shape[1]), bf16)
        for c in range(2):
            for k in range(X):
                weight = jnp.where(planall[c, k][:, i:i + 1] == dp, 1.0, 0.0).astype(bf16)
                result = result + arr[c, k] * weight
        placed_ref[i * brow:(i + 1) * brow, :] = result

    for copy in z_copies:
        copy.wait_recv()
    total = zf[ctx]
    for j in range(1, C):
        total = total + zrecv[j].astype(f32)
    full[dp, rep] = total
    ay_copies = [
        send(full.at[dp, rep], full.at[dp, rep], ay_s.at[j], ay_r.at[j], {"rep": (rep + j) % R})
        for j in range(1, R)
    ]
    for copy in ay_copies:
        copy.wait_recv()
    ad_copies = [
        send(full.at[dp], full.at[dp], ad_s.at[c, k], ad_r.at[c, k], {"dp": dp_to(c, k)}) for c, k in dp_peers
    ]
    for copy in ad_copies:
        copy.wait_recv()
    for d in range(DP):
        for r in range(R):
            for w in range(W // LANES):
                wg_ref[d * U + r * JJ:d * U + (r + 1) * JJ, w * LANES:(w + 1) * LANES] = full[
                    d, r, w * JJ:(w + 1) * JJ, :
                ]
    pending = [x_copies, p_copies, a_copies, gv_copies]
    for group in pending:
        for copy in group.values():
            copy.wait_send()
    for copy in y_copies + z_copies + ay_copies + ad_copies:
        copy.wait_send()


def local(inputs, queries, keys, values, grad_out, doc_ids, plan):
    DP, C, R = lax.axis_size("dp"), lax.axis_size("ctx"), lax.axis_size("rep")
    X = DP // 2
    T, D = inputs.shape[1:]
    QW, W = queries.shape[2], keys.shape[2]
    blocks = plan.shape[1]
    U = D // (DP * C)
    JJ, CC = U // R, LANES // U
    NB, rows = C // CC, C * U
    brow = T // blocks
    zrow = JJ * (W // LANES)
    bf16, f32, i32 = jnp.bfloat16, jnp.float32, jnp.int32
    vmem = pltpu.VMEM
    dma = pltpu.SemaphoreType.DMA
    spec = pl.BlockSpec(memory_space=pltpu.VMEM)

    def body(*refs):
        kernel((DP, C, R), *refs)

    placed, weight_grad = pl.pallas_call(
        body,
        out_shape=(jax.ShapeDtypeStruct((T, QW), bf16), jax.ShapeDtypeStruct((D // C, W), f32)),
        in_specs=[spec] * 6 + [pl.BlockSpec(memory_space=pltpu.SMEM)],
        out_specs=(spec, spec),
        scratch_shapes=[
            vmem((DP, LANES, CC * DP * U), bf16),
            vmem((DP, rows, T), bf16),
            vmem((2, X, rows, T), bf16),
            vmem((T, W), bf16),
            vmem((T, W), bf16),
            vmem((1, T), i32),
            vmem((KV_HEADS, GROUP * T, 2 * T), bf16),
            vmem((T, W), bf16),
            vmem((T, W), f32),
            vmem((T, W), bf16),
            vmem((2, X, T, W), bf16),
            vmem((T, QW), bf16),
            vmem((DP, brow, QW), bf16),
            vmem((2, X, brow, QW), bf16),
            vmem((1, LANES), i32),
            vmem((2, X, 1, LANES), i32),
            vmem((R, C * JJ, W), bf16),
            vmem((NB, LANES, W), f32),
            vmem((R, C * JJ, W), bf16),
            vmem((C, zrow, LANES), f32),
            vmem((C, zrow, LANES), bf16),
            vmem((C, zrow, LANES), bf16),
            vmem((DP, R, zrow, LANES), f32),
            dma((4,)), dma((4,)),
            dma((2, X)), dma((2, X)),
            dma((2, X)), dma((2, X)),
            dma((X,)), dma((X,)),
            dma((2, X)), dma((2, X)),
            dma((2, X)), dma((2, X)),
            dma((R,)), dma((R,)),
            dma((C,)), dma((C,)),
            dma((R,)), dma((R,)),
            dma((2, X)), dma((2, X)),
        ],
        compiler_params=pltpu.CompilerParams(
            collective_id=0, has_side_effects=True, vmem_limit_bytes=50 * 1024 * 1024
        ),
    )(inputs[0], queries[0], keys[0], values[0], grad_out[0], doc_ids, plan)
    return (placed[None], weight_grad)


def solution(mesh):
    tokens = P("dp", ("ctx", "rep"), None)
    marks = P("dp", ("ctx", "rep"))
    return jax.shard_map(
        local,
        mesh=mesh,
        in_specs=(tokens, tokens, tokens, tokens, tokens, marks, marks),
        out_specs=(tokens, P("ctx", None)),
        check_vma=False,
    )
```

time: 383 us -> 93.1 us (0.24); the launches traced: 377 us -> 92.7 us
  blocking collectives: 253 us -> 0 us
  Pallas kernels: 0 us -> 84.7 us
  waiting for transfers between devices: 56.5 us -> 0 us
  starting transfers between devices: 31 us -> 0 us
  between operations: 14.3 us -> 0.66 us
  matrix products: 10.8 us -> 0 us
    psum x1 -> x0, blocking collectives: 253 us -> none  [local(): weight_grad = lax.psum(partial_grad, ('dp', 'rep'))]
    pallas_call x0 -> x1, Pallas kernels: none -> 84.7 us  [local(): pl.pallas_call(body, out_shape=(jax.ShapeDtypeStruct((T, QW), bf16), jax....]
    reduce_scatter x1 -> x0, waiting for transfers between devices: 37.2 us -> none  [local(): lax.psum_scatter(jnp.einsum('tc,tf->cf', input_rows, grad_values, preferr...]
    all_to_all x2 -> x0, starting transfers between devices: 18.2 us -> none  [the longest x1 13.4 us: local(): lax.all_to_all(block_labels, 'dp', split_axis=0, concat_axis=0, tiled=True)]
    all_to_all x2 -> x0, waiting for transfers between devices: 14.9 us -> none  [the longest x1 14.9 us: local(): lax.all_to_all(outgoing, 'dp', split_axis=0, concat_axis=0, tiled=True)]
    ppermute x4 -> x0, starting transfers between devices: 12.8 us -> none  [from_behind(): return lax.ppermute(value, axis, pairs)]
    dot_general x5 -> x0, matrix products: 8.66 us -> none  [the longest x1 3.17 us: local(): jnp.einsum('tc,tf->cf', input_rows, grad_values, preferred_element_type=j...]
    ppermute x4 -> x0, waiting for transfers between devices: 4.39 us -> none  [from_behind(): return lax.ppermute(value, axis, pairs)]
  transfers between devices with their start and end apart: 7 -> 0, of which waited for: 3 -> 0; matrix products, arithmetic and copies ran while one was open for 3% -> 0% of each run, Pallas kernels for 0% -> 0%
where the time goes in v2:
time: 93.1 us; the launch traced here: 92.7 us
  Pallas kernels  84.7 us (91%)
  local copies, waits for them, and re-layouts  7.36 us (8%)
    pallas_call x1, Pallas kernels, local(): pl.pallas_call(body, out_shape=(jax.ShapeDtypeStruct((T, QW), bf16), jax....  84.7 us
    unnamed x16, local copies, waits for them, and re-layouts  7.36 us

profile of v2, /device:TPU:1, one launch (start us, length us, event | category | flops | bytes accessed | tf_op | source)
XLA Modules:
  0.0 92.7 jit_solution(4891098331729540447)
XLA Ops:
  0.6 0.0 copy-start.5
  0.6 0.0 copy-start.6
  0.7 0.6 copy-done.5
  1.3 0.0 copy-done.6
  1.3 0.0 copy-start
  1.3 1.2 %copy-done = bf16[1,128,4096]{2,1,0:T(8,128)(2,1)S(1)} copy-done((bf16[1,128,4096]{2,1,0:T(8,128)(2,1)S(1)}, bf16[1,128,4096]{2,1,0:T(8,128)(2,1)}, u32[]{:S(2)}) %copy-start) | copy-done | bytes 1048600
  2.5 0.0 copy-start.1
  2.5 1.0 %copy-done.1 = bf16[1,128,2048]{2,1,0:T(8,128)(2,1)S(1)} copy-done((bf16[1,128,2048]{2,1,0:T(8,128)(2,1)S(1)}, bf16[1,128,2048]{2,1,0:T(8,128)(2,1)}, u32[]{:S(2)}) %copy-start.1) | copy-done | bytes 524312
  3.6 0.0 copy-start.2
  3.6 1.0 %copy-done.2 = bf16[1,128,2048]{2,1,0:T(8,128)(2,1)S(1)} copy-done((bf16[1,128,2048]{2,1,0:T(8,128)(2,1)S(1)}, bf16[1,128,2048]{2,1,0:T(8,128)(2,1)}, u32[]{:S(2)}) %copy-start.2) | copy-done | bytes 524312
  4.6 0.0 copy-start.3
  4.6 0.9 copy-done.3
  5.5 0.0 copy-start.4
  5.5 0.9 copy-done.4
  6.4 84.7 %shard_map.86 = (bf16[128,2048]{1,0:T(8,128)(2,1)S(1)}, f32[256,512]{1,0:T(8,128)S(1)}) custom-call(bf16[128,4096]{1,0:T(8,128)(2,1)S(1)} %bitcast.6, bf16[128,2048]{1,0:T(8,128)(2,1)S(1)} %bitcast.8, bf16[128,512]{1,0:T(8,128)(2,1)S(1)} %bitcast.10, bf16[128,512]{1,0:T(8,128)(2,1)S(1)} %bitcast.11, bf16[128,2048]{1,0:T(8,128)(2,1)S(1)} %bitcast.9, ...), custom_call_target="tpu_custom_call" | custom-call | tf_op jit(solution)/shard_map/pallas_call | solution.py:266
  91.1 0.8 copy.11
  91.9 0.8 copy.12
Async XLA Ops:
  0.6 0.7 copy-start.5
  0.6 0.7 copy-start.6
  1.3 1.2 %copy-start = (bf16[1,128,4096]{2,1,0:T(8,128)(2,1)S(1)}, bf16[1,128,4096]{2,1,0:T(8,128)(2,1)}, u32[]{:S(2)}) copy-start(bf16[1,128,4096]{2,1,0:T(8,128)(2,1)} %param.7) | copy-start | bytes 3145732
  2.5 1.0 %copy-start.1 = (bf16[1,128,2048]{2,1,0:T(8,128)(2,1)S(1)}, bf16[1,128,2048]{2,1,0:T(8,128)(2,1)}, u32[]{:S(2)}) copy-start(bf16[1,128,2048]{2,1,0:T(8,128)(2,1)} %param.8) | copy-start | bytes 1572868
  3.6 1.0 %copy-start.2 = (bf16[1,128,2048]{2,1,0:T(8,128)(2,1)S(1)}, bf16[1,128,2048]{2,1,0:T(8,128)(2,1)}, u32[]{:S(2)}) copy-start(bf16[1,128,2048]{2,1,0:T(8,128)(2,1)} %param.11) | copy-start | bytes 1572868
  4.6 0.9 copy-start.3
  5.5 0.9 copy-start.4

commit v3 on v2

--- a/solution.py
+++ b/solution.py
@@ -16,17 +16,17 @@
 
 def kernel(
     sizes,
-    x_ref, q_ref, k_ref, v_ref, g_ref, docs_ref, plan_ref,
-    placed_ref, wg_ref,
-    perm, xs, xg, kprev, vprev, docprev, probs, dvp, dvo, dvr, gvg, att, slots, arr,
+    x_hbm, q_hbm, k_hbm, v_hbm, g_hbm, docs_ref, plan_ref,
+    placed_hbm, wg_ref,
+    placed_ref, x_ref, q_ref, k_ref, v_ref, g_ref, perm, xs, xg, kprev, vprev, docprev, probs, dvp, dvo, dvr, gvg, att, slots, arr,
     planrow, planall, ysend, yown, yrecv, zf, zsend, zrecv, full,
     nb_s, nb_r, x_s, x_r, gv_s, gv_r, gf_s, gf_r, a_s, a_r, p_s, p_r,
-    y_s, y_r, z_s, z_r, ay_s, ay_r, ad_s, ad_r,
+    y_s, y_r, z_s, z_r, ay_s, ay_r, ad_s, ad_r, in_s, out_s,
 ):
     DP, C, R = sizes
     X = DP // 2
-    T, D = x_ref.shape
-    W = k_ref.shape[1]
+    T, D = x_hbm.shape
+    W = k_hbm.shape[1]
     blocks = plan_ref.shape[1]
     brow = T // blocks
     U = D // (DP * C)
@@ -62,6 +62,15 @@
     for j in range(1, C):
         greet({"ctx": (ctx + j) % C})
 
+    loads = [
+        pltpu.make_async_copy(src, dst, in_s.at[i])
+        for i, (src, dst) in enumerate(
+            [(k_hbm, k_ref), (x_hbm, x_ref), (v_hbm, v_ref), (q_hbm, q_ref), (g_hbm, g_ref)]
+        )
+    ]
+    for load in loads:
+        load.start()
+
     def send(src, dst, ssem, rsem, device):
         copy = pltpu.make_async_remote_copy(
             src_ref=src, dst_ref=dst, send_sem=ssem, recv_sem=rsem, device_id=device, device_id_type=MESH
@@ -83,14 +92,15 @@
         column = lax.broadcasted_iota(jnp.int32, (LANES, width), 1)
         perm[d] = jnp.where(column == source, 1.0, 0.0).astype(bf16)
 
+    for load in loads:
+        load.wait()
     pl.semaphore_wait(barrier, 2 + (DP - 1) + (R - 1) + (C - 1))
 
-    pending = []
     near = [
         send(k_ref, kprev, nb_s.at[0], nb_r.at[0], next_dev),
-        send(v_ref, vprev, nb_s.at[1], nb_r.at[1], next_dev),
         send(docs_ref, docprev, nb_s.at[2], nb_r.at[2], next_dev),
     ]
+    v_copy = send(v_ref, vprev, nb_s.at[1], nb_r.at[1], next_dev)
 
     for b in range(NB):
         for d in range(DP):
@@ -136,6 +146,7 @@
         dvo[:, cols] = dv[T:]
     dv_copy = send(dvp, dvr, nb_s.at[3], nb_r.at[3], prev_dev)
 
+    v_copy.wait()
     for g in range(KV_HEADS):
         cols = slice(g * HEAD_DIM, (g + 1) * HEAD_DIM)
         vals = jnp.concatenate([vprev[:, cols], v_ref[:, cols]], axis=0)
@@ -143,42 +154,52 @@
         for h in range(GROUP):
             att[:, (g * GROUP + h) * HEAD_DIM:(g * GROUP + h + 1) * HEAD_DIM] = out[h * T:(h + 1) * T]
 
-    dv_copy.wait()
-    gvg[0, 0] = (dvo[...] + dvr[...].astype(f32)).astype(bf16)
-    gv_copies = {}
-    for c, k in [(1, 0)] + [(0, k) for k in range(1, X)]:
-        gv_copies[c, k] = send(gvg.at[0, 0], gvg.at[c, k], gv_s.at[c, k], gv_r.at[c, k], {"dp": dp_to(c, k)})
-
     for p in range(DP):
         slot = jnp.zeros((brow, att.shape[1]), bf16)
         for i in range(blocks):
             weight = jnp.where(plan_ref[0, i] == p, 1.0, 0.0).astype(f32)
             slot = slot + att[i * brow:(i + 1) * brow, :] * jnp.full((1, 1), weight, f32).astype(bf16)
         slots[p] = slot
+
+    dv_copy.wait()
+    gvg[0, 0] = (dvo[...] + dvr[...].astype(f32)).astype(bf16)
+    gv_copies = {}
+    for c, k in [(1, 0)] + [(0, k) for k in range(1, X)]:
+        gv_copies[c, k] = send(gvg.at[0, 0], gvg.at[c, k], gv_s.at[c, k], gv_r.at[c, k], {"dp": dp_to(c, k)})
+
     a_copies = {}
     for c, k in dp_peers:
         a_copies[c, k] = send(
             slots.at[dp_to(c, k)], arr.at[c, k], a_s.at[c, k], a_r.at[c, k], {"dp": dp_to(c, k)}
         )
 
-    for k in range(1, X):
+    def accumulate(members, first=False, last=False):
+        for b in range(NB):
+            rows = slice(b * LANES, (b + 1) * LANES)
+            part = None if first else yown[b]
+            for c, k in members:
+                term = jnp.dot(xg[c, k, rows, :], gvg[c, k], preferred_element_type=f32)
+                part = term if part is None else part + term
+            yown[b] = part
+            if last:
+                for r in range(R):
+                    ysend[r, b * CH:(b + 1) * CH, :] = part[r * CH:(r + 1) * CH].astype(bf16)
+
+    x_copies[1, 0].wait_recv()
+    gv_copies[1, 0].wait_recv()
+    accumulate([(0, 0), (1, 0)], first=True, last=X == 1)
+    nearest = sorted(range(1, X), key=lambda k: min(k, X - k))
+    for k in nearest:
         gv_copies[0, k].wait_recv()
         gv_copies[1, k] = send(gvg.at[0, k], gvg.at[1, k], gf_s.at[k], gf_r.at[k], {"dp": dp_to(1, 0)})
-    for c, k in dp_peers:
-        x_copies[c, k].wait_recv()
-    gv_copies[1, 0].wait_recv()
-    for k in range(1, X):
-        gv_copies[1, k].wait_recv()
-
-    for b in range(NB):
-        rows = slice(b * LANES, (b + 1) * LANES)
-        part = jnp.zeros((LANES, W), f32)
-        for c in range(2):
-            for k in range(X):
-                part = part + jnp.dot(xg[c, k, rows, :], gvg[c, k], preferred_element_type=f32)
-        yown[b] = part
-        for r in range(R):
-            ysend[r, b * CH:(b + 1) * CH, :] = part[r * CH:(r + 1) * CH].astype(bf16)
+    for k in nearest:
+        x_copies[0, k].wait_recv()
+        x_copies[1, k].wait_recv()
+    if X > 1:
+        accumulate([(0, k) for k in nearest])
+        for k in nearest:
+            gv_copies[1, k].wait_recv()
+        accumulate([(1, k) for k in nearest], last=True)
     y_copies = [
         send(ysend.at[(rep + j) % R], yrecv.at[j], y_s.at[j], y_r.at[j], {"rep": (rep + j) % R})
         for j in range(1, R)
@@ -212,22 +233,28 @@
                 weight = jnp.where(planall[c, k][:, i:i + 1] == dp, 1.0, 0.0).astype(bf16)
                 result = result + arr[c, k] * weight
         placed_ref[i * brow:(i + 1) * brow, :] = result
+    store = pltpu.make_async_copy(placed_ref, placed_hbm, out_s)
+    store.start()
 
     for copy in z_copies:
         copy.wait_recv()
     total = zf[ctx]
     for j in range(1, C):
         total = total + zrecv[j].astype(f32)
-    full[dp, rep] = total
+    full[dp, rep] = total.astype(bf16)
     ay_copies = [
         send(full.at[dp, rep], full.at[dp, rep], ay_s.at[j], ay_r.at[j], {"rep": (rep + j) % R})
         for j in range(1, R)
     ]
-    for copy in ay_copies:
-        copy.wait_recv()
-    ad_copies = [
-        send(full.at[dp], full.at[dp], ad_s.at[c, k], ad_r.at[c, k], {"dp": dp_to(c, k)}) for c, k in dp_peers
-    ]
+    ad_copies = []
+    for j in [0] + sorted(range(1, R), key=lambda j: min(j, R - j)):
+        if j:
+            ay_copies[j - 1].wait_recv()
+        piece = full.at[dp, (rep + R - j) % R]
+        for c, k in dp_peers:
+            ad_copies.append(
+                send(piece, piece, ad_s.at[j, c, k], ad_r.at[j, c, k], {"dp": dp_to(c, k)})
+            )
     for copy in ad_copies:
         copy.wait_recv()
     for d in range(DP):
@@ -235,9 +262,9 @@
             for w in range(W // LANES):
                 wg_ref[d * U + r * JJ:d * U + (r + 1) * JJ, w * LANES:(w + 1) * LANES] = full[
                     d, r, w * JJ:(w + 1) * JJ, :
-                ]
-    pending = [x_copies, p_copies, a_copies, gv_copies]
-    for group in pending:
+                ].astype(f32)
+    store.wait()
+    for group in (x_copies, p_copies, a_copies, gv_copies):
         for copy in group.values():
             copy.wait_send()
     for copy in y_copies + z_copies + ay_copies + ad_copies:
@@ -266,9 +293,15 @@
     placed, weight_grad = pl.pallas_call(
         body,
         out_shape=(jax.ShapeDtypeStruct((T, QW), bf16), jax.ShapeDtypeStruct((D // C, W), f32)),
-        in_specs=[spec] * 6 + [pl.BlockSpec(memory_space=pltpu.SMEM)],
-        out_specs=(spec, spec),
+        in_specs=[pl.BlockSpec(memory_space=pltpu.HBM)] * 5 + [spec] + [pl.BlockSpec(memory_space=pltpu.SMEM)],
+        out_specs=(pl.BlockSpec(memory_space=pltpu.HBM), spec),
         scratch_shapes=[
+            vmem((T, QW), bf16),
+            vmem((T, D), bf16),
+            vmem((T, QW), bf16),
+            vmem((T, W), bf16),
+            vmem((T, W), bf16),
+            vmem((T, QW), bf16),
             vmem((DP, LANES, CC * DP * U), bf16),
             vmem((DP, rows, T), bf16),
             vmem((2, X, rows, T), bf16),
@@ -291,7 +324,7 @@
             vmem((C, zrow, LANES), f32),
             vmem((C, zrow, LANES), bf16),
             vmem((C, zrow, LANES), bf16),
-            vmem((DP, R, zrow, LANES), f32),
+            vmem((DP, R, zrow, LANES), bf16),
             dma((4,)), dma((4,)),
             dma((2, X)), dma((2, X)),
             dma((2, X)), dma((2, X)),
@@ -301,10 +334,11 @@
             dma((R,)), dma((R,)),
             dma((C,)), dma((C,)),
             dma((R,)), dma((R,)),
-            dma((2, X)), dma((2, X)),
+            dma((R, 2, X)), dma((R, 2, X)),
+            dma((5,)), dma,
         ],
         compiler_params=pltpu.CompilerParams(
-            collective_id=0, has_side_effects=True, vmem_limit_bytes=50 * 1024 * 1024
+            collective_id=0, has_side_effects=True, vmem_limit_bytes=67_000_000
         ),
     )(inputs[0], queries[0], keys[0], values[0], grad_out[0], doc_ids, plan)
     return (placed[None], weight_grad)

time: 93.1 us -> 86.6 us (0.930)
  local copies, waits for them, and re-layouts: 7.36 us -> 2.74 us
  Pallas kernels: 84.7 us -> 83 us
    unnamed x16 -> x4, local copies, waits for them, and re-layouts: 7.36 us -> 2.74 us
    pallas_call x1, Pallas kernels: 84.7 us -> 83 us  [local(): pl.pallas_call(body, out_shape=(jax.ShapeDtypeStruct((T, QW), bf16), jax....]
where the time goes in v3:
time: 86.6 us; the launch traced here: 86.4 us
  Pallas kernels  83 us (96%)
  local copies, waits for them, and re-layouts  2.74 us (3%)
    pallas_call x1, Pallas kernels, local(): pl.pallas_call(body, out_shape=(jax.ShapeDtypeStruct((T, QW), bf16), jax....  83 us
    unnamed x4, local copies, waits for them, and re-layouts  2.74 us

profile of v3, /device:TPU:1, one launch (start us, length us, event | category | flops | bytes accessed | tf_op | source)
XLA Modules:
  0.0 86.4 jit_solution(1206785271757590427)
XLA Ops:
  0.6 83.0 %shard_map.86 = (bf16[128,2048]{1,0:T(8,128)(2,1)}, f32[256,512]{1,0:T(8,128)}) custom-call(bf16[128,4096]{1,0:T(8,128)(2,1)} %bitcast.6, bf16[128,2048]{1,0:T(8,128)(2,1)} %bitcast.8, bf16[128,512]{1,0:T(8,128)(2,1)} %bitcast.10, bf16[128,512]{1,0:T(8,128)(2,1)} %bitcast.11, bf16[128,2048]{1,0:T(8,128)(2,1)} %bitcast.9, s32[1,128]{1,0:T(1,128)} %refs_5_.1, ...), custom_call_target="tpu_custom_call" | custom-call | tf_op jit(solution)/shard_map/pallas_call | solution.py:293
  83.6 0.0 copy-start
  83.6 1.9 %copy.11 = bf16[1,128,2048]{2,1,0:T(8,128)(2,1)} copy(bf16[1,128,2048]{2,1,0:T(8,128)(2,1)} %bitcast.7) | data formatting | bytes 1048576
  85.6 0.0 copy-done
  85.6 0.8 copy.12
Async XLA Ops:
  83.6 2.0 %copy-start = (f32[256,512]{1,0:T(8,128)S(1)}, f32[256,512]{1,0:T(8,128)}, u32[]{:S(2)}) copy-start(f32[256,512]{1,0:T(8,128)} %get-tuple-element.9) | copy-start | bytes 1572868

commit v4 on v3

--- a/solution.py
+++ b/solution.py
@@ -19,9 +19,9 @@
     x_hbm, q_hbm, k_hbm, v_hbm, g_hbm, docs_ref, plan_ref,
     placed_hbm, wg_ref,
     placed_ref, x_ref, q_ref, k_ref, v_ref, g_ref, perm, xs, xg, kprev, vprev, docprev, probs, dvp, dvo, dvr, gvg, att, slots, arr,
-    planrow, planall, ysend, yown, yrecv, zf, zsend, zrecv, full,
+    planrow, planall, ysend, yown, yrecv, zf, zsend, zrecv, zbf, zbsend, zbrecv, ybf, ybrecv, full,
     nb_s, nb_r, x_s, x_r, gv_s, gv_r, gf_s, gf_r, a_s, a_r, p_s, p_r,
-    y_s, y_r, z_s, z_r, ay_s, ay_r, ad_s, ad_r, in_s, out_s,
+    y_s, y_r, z_s, z_r, ay_s, ay_r, ad_s, ad_r, zb_s, zb_r, yb_s, yb_r, in_s, out_s,
 ):
     DP, C, R = sizes
     X = DP // 2
@@ -34,6 +34,8 @@
     CC = LANES // U
     NB = C // CC
     CH = CC * JJ
+    WA = W - LANES
+    ZA = JJ * (WA // LANES)
     f32, bf16 = jnp.float32, jnp.bfloat16
 
     dp, ctx, rep = lax.axis_index("dp"), lax.axis_index("ctx"), lax.axis_index("rep")
@@ -84,6 +86,8 @@
         row = jnp.where(lane == i, plan_ref[0, i], row)
     planrow[...] = row
 
+    zf[...] = jnp.zeros_like(zf)
+    ybf[...] = jnp.zeros_like(ybf)
     width = CC * DP * U
     for d in range(DP):
         o = lax.broadcasted_iota(jnp.int32, (LANES, 1), 0)
@@ -94,20 +98,20 @@
 
     for load in loads:
         load.wait()
-    pl.semaphore_wait(barrier, 2 + (DP - 1) + (R - 1) + (C - 1))
-
-    near = [
-        send(k_ref, kprev, nb_s.at[0], nb_r.at[0], next_dev),
-        send(docs_ref, docprev, nb_s.at[2], nb_r.at[2], next_dev),
-    ]
-    v_copy = send(v_ref, vprev, nb_s.at[1], nb_r.at[1], next_dev)
-
     for b in range(NB):
         for d in range(DP):
             xs[d, b * LANES:(b + 1) * LANES, :] = lax.dot_general(
                 perm[d], x_ref[:, b * width:(b + 1) * width], (((1,), (1,)), ((), ())),
                 preferred_element_type=f32,
             ).astype(bf16)
+    pl.semaphore_wait(barrier, 2 + (DP - 1) + (R - 1) + (C - 1))
+
+    near = [
+        send(k_ref, kprev, nb_s.at[0], nb_r.at[0], next_dev),
+        send(docs_ref, docprev, nb_s.at[2], nb_r.at[2], next_dev),
+    ]
+    v_copy = send(v_ref, vprev, nb_s.at[1], nb_r.at[1], next_dev)
+
     x_copies, p_copies = {}, {}
     for c, k in dp_peers:
         to = {"dp": dp_to(c, k)}
@@ -183,7 +187,11 @@
             yown[b] = part
             if last:
                 for r in range(R):
-                    ysend[r, b * CH:(b + 1) * CH, :] = part[r * CH:(r + 1) * CH].astype(bf16)
+                    ysend[r, b * CH:(b + 1) * CH, :] = part[r * CH:(r + 1) * CH, :WA].astype(bf16)
+                    for cc in range(CC):
+                        zbf[b * CC + cc, r * JJ:(r + 1) * JJ, :] = part[
+                            r * CH + cc * JJ:r * CH + (cc + 1) * JJ, WA:
+                        ]
 
     x_copies[1, 0].wait_recv()
     gv_copies[1, 0].wait_recv()
@@ -204,14 +212,19 @@
         send(ysend.at[(rep + j) % R], yrecv.at[j], y_s.at[j], y_r.at[j], {"rep": (rep + j) % R})
         for j in range(1, R)
     ]
+    zbsend[...] = zbf[...].astype(bf16)
+    zb_copies = [
+        send(zbsend.at[(ctx + j) % C], zbrecv.at[j], zb_s.at[j], zb_r.at[j], {"ctx": (ctx + j) % C})
+        for j in range(1, C)
+    ]
     for copy in y_copies:
         copy.wait_recv()
     for b in range(NB):
-        total = yown[b, pl.ds(pl.multiple_of(rep * CH, CH), CH), :]
+        total = yown[b, pl.ds(pl.multiple_of(rep * CH, CH), CH), :WA]
         for j in range(1, R):
             total = total + yrecv[j, b * CH:(b + 1) * CH, :].astype(f32)
         for cc in range(CC):
-            for w in range(W // LANES):
+            for w in range(WA // LANES):
                 zf[b * CC + cc, w * JJ:(w + 1) * JJ, :] = total[
                     cc * JJ:(cc + 1) * JJ, w * LANES:(w + 1) * LANES
                 ]
@@ -221,6 +234,17 @@
         for j in range(1, C)
     ]
 
+    for copy in zb_copies:
+        copy.wait_recv()
+    total = zbf[ctx]
+    for j in range(1, C):
+        total = total + zbrecv[j].astype(f32)
+    for r in range(R):
+        ybf[r, :JJ, :] = total[r * JJ:(r + 1) * JJ]
+    yb_copies = [
+        send(ybf.at[(rep + j) % R], ybrecv.at[j], yb_s.at[j], yb_r.at[j], {"rep": (rep + j) % R})
+        for j in range(1, R)
+    ]
     for c, k in dp_peers:
         p_copies[c, k].wait_recv()
         a_copies[c, k].wait_recv()
@@ -241,7 +265,12 @@
     total = zf[ctx]
     for j in range(1, C):
         total = total + zrecv[j].astype(f32)
-    full[dp, rep] = total.astype(bf16)
+    for copy in yb_copies:
+        copy.wait_recv()
+    total_b = ybf[rep]
+    for j in range(1, R):
+        total_b = total_b + ybrecv[j]
+    full[dp, rep] = jnp.concatenate([total[:ZA], total_b[:JJ]], axis=0).astype(bf16)
     ay_copies = [
         send(full.at[dp, rep], full.at[dp, rep], ay_s.at[j], ay_r.at[j], {"rep": (rep + j) % R})
         for j in range(1, R)
@@ -267,7 +296,7 @@
     for group in (x_copies, p_copies, a_copies, gv_copies):
         for copy in group.values():
             copy.wait_send()
-    for copy in y_copies + z_copies + ay_copies + ad_copies:
+    for copy in y_copies + z_copies + zb_copies + yb_copies + ay_copies + ad_copies:
         copy.wait_send()
 
 
@@ -318,12 +347,17 @@
             vmem((2, X, brow, QW), bf16),
             vmem((1, LANES), i32),
             vmem((2, X, 1, LANES), i32),
-            vmem((R, C * JJ, W), bf16),
+            vmem((R, C * JJ, W - LANES), bf16),
             vmem((NB, LANES, W), f32),
-            vmem((R, C * JJ, W), bf16),
+            vmem((R, C * JJ, W - LANES), bf16),
             vmem((C, zrow, LANES), f32),
             vmem((C, zrow, LANES), bf16),
             vmem((C, zrow, LANES), bf16),
+            vmem((C, U, LANES), f32),
+            vmem((C, U, LANES), bf16),
+            vmem((C, U, LANES), bf16),
+            vmem((R, max(JJ, 8), LANES), f32),
+            vmem((R, max(JJ, 8), LANES), f32),
             vmem((DP, R, zrow, LANES), bf16),
             dma((4,)), dma((4,)),
             dma((2, X)), dma((2, X)),
@@ -335,6 +369,8 @@
             dma((C,)), dma((C,)),
             dma((R,)), dma((R,)),
             dma((R, 2, X)), dma((R, 2, X)),
+            dma((C,)), dma((C,)),
+            dma((R,)), dma((R,)),
             dma((5,)), dma,
         ],
         compiler_params=pltpu.CompilerParams(

time: 86.6 us -> 83.1 us (0.960)
  Pallas kernels: 83 us -> 79.5 us
    pallas_call x1, Pallas kernels: 83 us -> 79.5 us  [local(): pl.pallas_call(body, out_shape=(jax.ShapeDtypeStruct((T, QW), bf16), jax....]
where the time goes in v4:
time: 83.1 us; the launch traced here: 82.9 us
  Pallas kernels  79.5 us (96%)
  local copies, waits for them, and re-layouts  2.74 us (3%)
    pallas_call x1, Pallas kernels, local(): pl.pallas_call(body, out_shape=(jax.ShapeDtypeStruct((T, QW), bf16), jax....  79.5 us
    unnamed x4, local copies, waits for them, and re-layouts  2.74 us

profile of v4, /device:TPU:1, one launch (start us, length us, event | category | flops | bytes accessed | tf_op | source)
XLA Modules:
  0.0 82.9 jit_solution(8062085709868060731)
XLA Ops:
  0.6 79.5 %shard_map.86 = (bf16[128,2048]{1,0:T(8,128)(2,1)}, f32[256,512]{1,0:T(8,128)}) custom-call(bf16[128,4096]{1,0:T(8,128)(2,1)} %bitcast.6, bf16[128,2048]{1,0:T(8,128)(2,1)} %bitcast.8, bf16[128,512]{1,0:T(8,128)(2,1)} %bitcast.10, bf16[128,512]{1,0:T(8,128)(2,1)} %bitcast.11, bf16[128,2048]{1,0:T(8,128)(2,1)} %bitcast.9, s32[1,128]{1,0:T(1,128)} %refs_5_.1, ...), custom_call_target="tpu_custom_call" | custom-call | tf_op jit(solution)/shard_map/pallas_call | solution.py:322
  80.1 0.0 copy-start
  80.1 1.9 %copy.11 = bf16[1,128,2048]{2,1,0:T(8,128)(2,1)} copy(bf16[1,128,2048]{2,1,0:T(8,128)(2,1)} %bitcast.7) | data formatting | bytes 1048576
  82.1 0.0 copy-done
  82.1 0.8 copy.12
Async XLA Ops:
  80.1 2.0 %copy-start = (f32[256,512]{1,0:T(8,128)S(1)}, f32[256,512]{1,0:T(8,128)}, u32[]{:S(2)}) copy-start(f32[256,512]{1,0:T(8,128)} %get-tuple-element.9) | copy-start | bytes 1572868

commit v5 on v4

--- a/solution.py
+++ b/solution.py
@@ -21,7 +21,7 @@
     placed_ref, x_ref, q_ref, k_ref, v_ref, g_ref, perm, xs, xg, kprev, vprev, docprev, probs, dvp, dvo, dvr, gvg, att, slots, arr,
     planrow, planall, ysend, yown, yrecv, zf, zsend, zrecv, zbf, zbsend, zbrecv, ybf, ybrecv, full,
     nb_s, nb_r, x_s, x_r, gv_s, gv_r, gf_s, gf_r, a_s, a_r, p_s, p_r,
-    y_s, y_r, z_s, z_r, ay_s, ay_r, ad_s, ad_r, zb_s, zb_r, yb_s, yb_r, in_s, out_s,
+    y_s, y_r, z_s, z_r, ay_s, ay_r, ad_s, ad_r, zb_s, zb_r, yb_s, yb_r, in_s, out_s, wide,
 ):
     DP, C, R = sizes
     X = DP // 2
@@ -59,10 +59,25 @@
     greet(prev_dev)
     for c, k in dp_peers:
         greet({"dp": dp_to(c, k)})
-    for j in range(1, R):
+    near_rep, near_ctx = sorted({1 % R, R - 1} - {0}), sorted({1 % C, C - 1} - {0})
+    for j in near_rep:
         greet({"rep": (rep + j) % R})
-    for j in range(1, C):
+    for j in near_ctx:
         greet({"ctx": (ctx + j) % C})
+
+    def widen(step):
+        for i, (axis, at, n) in enumerate((("rep", rep, R), ("ctx", ctx, C))):
+            reach = 2 ** step
+            if 2 * reach < n:
+                for j in (reach, n - reach):
+                    pl.semaphore_signal(
+                        wide.at[i, step], inc=1, device_id={axis: (at + j) % n}, device_id_type=MESH
+                    )
+
+    def widened(step):
+        for i, n in enumerate((R, C)):
+            if 2 * 2 ** step < n:
+                pl.semaphore_wait(wide.at[i, step], 2)
 
     loads = [
         pltpu.make_async_copy(src, dst, in_s.at[i])
@@ -104,7 +119,7 @@
                 perm[d], x_ref[:, b * width:(b + 1) * width], (((1,), (1,)), ((), ())),
                 preferred_element_type=f32,
             ).astype(bf16)
-    pl.semaphore_wait(barrier, 2 + (DP - 1) + (R - 1) + (C - 1))
+    pl.semaphore_wait(barrier, 2 + (DP - 1) + len(near_rep) + len(near_ctx))
 
     near = [
         send(k_ref, kprev, nb_s.at[0], nb_r.at[0], next_dev),
@@ -118,6 +133,7 @@
         p_copies[c, k] = send(planrow, planall.at[c, k], p_s.at[c, k], p_r.at[c, k], to)
         x_copies[c, k] = send(xs.at[dp_to(c, k)], xg.at[c, k], x_s.at[c, k], x_r.at[c, k], to)
     xg[0, 0] = xs[dp]
+    widen(0)
 
     docs = docs_ref[...].astype(f32)
     by_row = jnp.broadcast_to(docs, (T, T)).T
@@ -126,6 +142,8 @@
     own = jnp.where((by_row == docs) & (u_pos <= t_pos), 1.0, 0.0)
     for copy in near:
         copy.wait()
+    widened(0)
+    widen(1)
     prior = jnp.where(by_row == docprev[...].astype(f32), 1.0, 0.0) * jnp.where(shard > 0, 1.0, 0.0)
     allowed = jnp.concatenate([prior, own], axis=1)
     allowed = jnp.concatenate([allowed] * GROUP, axis=0) > 0.5
@@ -135,6 +153,7 @@
             [ref[:, (g * GROUP + h) * HEAD_DIM:(g * GROUP + h + 1) * HEAD_DIM] for h in range(GROUP)], axis=0
         )
 
+    dv_copies = []
     for g in range(KV_HEADS):
         cols = slice(g * HEAD_DIM, (g + 1) * HEAD_DIM)
         keys = jnp.concatenate([kprev[:, cols], k_ref[:, cols]], axis=0)
@@ -148,7 +167,13 @@
         dv = lax.dot_general(p, heads(g_ref, g), (((0,), (0,)), ((), ())), preferred_element_type=f32)
         dvp[:, cols] = dv[:T].astype(bf16)
         dvo[:, cols] = dv[T:]
-    dv_copy = send(dvp, dvr, nb_s.at[3], nb_r.at[3], prev_dev)
+        if g % 2:
+            pair = pl.ds((g - 1) * HEAD_DIM, 2 * HEAD_DIM)
+            dv_copies.append(
+                send(dvp.at[:, pair], dvr.at[:, pair], nb_s.at[3 + g // 2], nb_r.at[3 + g // 2], prev_dev)
+            )
+    widened(1)
+    widen(2)
 
     v_copy.wait()
     for g in range(KV_HEADS):
@@ -165,7 +190,8 @@
             slot = slot + att[i * brow:(i + 1) * brow, :] * jnp.full((1, 1), weight, f32).astype(bf16)
         slots[p] = slot
 
-    dv_copy.wait()
+    for copy in dv_copies:
+        copy.wait()
     gvg[0, 0] = (dvo[...] + dvr[...].astype(f32)).astype(bf16)
     gv_copies = {}
     for c, k in [(1, 0)] + [(0, k) for k in range(1, X)]:
@@ -176,6 +202,8 @@
         a_copies[c, k] = send(
             slots.at[dp_to(c, k)], arr.at[c, k], a_s.at[c, k], a_r.at[c, k], {"dp": dp_to(c, k)}
         )
+
+    widened(2)
 
     def accumulate(members, first=False, last=False):
         for b in range(NB):
@@ -359,7 +387,7 @@
             vmem((R, max(JJ, 8), LANES), f32),
             vmem((R, max(JJ, 8), LANES), f32),
             vmem((DP, R, zrow, LANES), bf16),
-            dma((4,)), dma((4,)),
+            dma((5,)), dma((5,)),
             dma((2, X)), dma((2, X)),
             dma((2, X)), dma((2, X)),
             dma((X,)), dma((X,)),
@@ -372,6 +400,7 @@
             dma((C,)), dma((C,)),
             dma((R,)), dma((R,)),
             dma((5,)), dma,
+            pltpu.SemaphoreType.REGULAR((2, 3)),
         ],
         compiler_params=pltpu.CompilerParams(
             collective_id=0, has_side_effects=True, vmem_limit_bytes=67_000_000

time: 83.1 us -> 80.2 us (0.965)
  Pallas kernels: 79.5 us -> 76.6 us
    pallas_call x1, Pallas kernels: 79.5 us -> 76.6 us  [local(): pl.pallas_call(body, out_shape=(jax.ShapeDtypeStruct((T, QW), bf16), jax....]
where the time goes in v5:
time: 80.2 us; the launch traced here: 80 us
  Pallas kernels  76.6 us (96%)
  local copies, waits for them, and re-layouts  2.74 us (3%)
    pallas_call x1, Pallas kernels, local(): pl.pallas_call(body, out_shape=(jax.ShapeDtypeStruct((T, QW), bf16), jax....  76.6 us
    unnamed x4, local copies, waits for them, and re-layouts  2.74 us

profile of v5, /device:TPU:1, one launch (start us, length us, event | category | flops | bytes accessed | tf_op | source)
XLA Modules:
  0.0 80.0 jit_solution(12737044045944767187)
XLA Ops:
  0.6 76.6 %shard_map.86 = (bf16[128,2048]{1,0:T(8,128)(2,1)}, f32[256,512]{1,0:T(8,128)}) custom-call(bf16[128,4096]{1,0:T(8,128)(2,1)} %bitcast.6, bf16[128,2048]{1,0:T(8,128)(2,1)} %bitcast.8, bf16[128,512]{1,0:T(8,128)(2,1)} %bitcast.10, bf16[128,512]{1,0:T(8,128)(2,1)} %bitcast.11, bf16[128,2048]{1,0:T(8,128)(2,1)} %bitcast.9, s32[1,128]{1,0:T(1,128)} %refs_5_.1, ...), custom_call_target="tpu_custom_call" | custom-call | tf_op jit(solution)/shard_map/pallas_call | solution.py:350
  77.2 0.0 copy-start
  77.2 1.9 %copy.11 = bf16[1,128,2048]{2,1,0:T(8,128)(2,1)} copy(bf16[1,128,2048]{2,1,0:T(8,128)(2,1)} %bitcast.7) | data formatting | bytes 1048576
  79.2 0.0 copy-done
  79.2 0.8 copy.12
Async XLA Ops:
  77.2 2.0 %copy-start = (f32[256,512]{1,0:T(8,128)S(1)}, f32[256,512]{1,0:T(8,128)}, u32[]{:S(2)}) copy-start(f32[256,512]{1,0:T(8,128)} %get-tuple-element.9) | copy-start | bytes 1572868

commit v6 on v5

--- a/solution.py
+++ b/solution.py
@@ -48,7 +48,10 @@
     def dp_to(c, k):
         return ((chip + k) % X) * 2 + (core + c) % 2
 
-    dp_peers = [(c, k) for c in range(2) for k in range(X) if (c, k) != (0, 0)]
+    def far_first(n):
+        return sorted(range(1, n), key=lambda j: -min(j, n - j))
+
+    dp_peers = [(c, k) for k in far_first(X) + [0] for c in range(2) if (c, k) != (0, 0)]
 
     barrier = pltpu.get_barrier_semaphore()
 
@@ -194,7 +197,7 @@
         copy.wait()
     gvg[0, 0] = (dvo[...] + dvr[...].astype(f32)).astype(bf16)
     gv_copies = {}
-    for c, k in [(1, 0)] + [(0, k) for k in range(1, X)]:
+    for c, k in [(1, 0)] + [(0, k) for k in far_first(X)]:
         gv_copies[c, k] = send(gvg.at[0, 0], gvg.at[c, k], gv_s.at[c, k], gv_r.at[c, k], {"dp": dp_to(c, k)})
 
     a_copies = {}
@@ -238,12 +241,12 @@
         accumulate([(1, k) for k in nearest], last=True)
     y_copies = [
         send(ysend.at[(rep + j) % R], yrecv.at[j], y_s.at[j], y_r.at[j], {"rep": (rep + j) % R})
-        for j in range(1, R)
+        for j in far_first(R)
     ]
     zbsend[...] = zbf[...].astype(bf16)
     zb_copies = [
         send(zbsend.at[(ctx + j) % C], zbrecv.at[j], zb_s.at[j], zb_r.at[j], {"ctx": (ctx + j) % C})
-        for j in range(1, C)
+        for j in far_first(C)
     ]
     for copy in y_copies:
         copy.wait_recv()
@@ -259,7 +262,7 @@
     zsend[...] = zf[...].astype(bf16)
     z_copies = [
         send(zsend.at[(ctx + j) % C], zrecv.at[j], z_s.at[j], z_r.at[j], {"ctx": (ctx + j) % C})
-        for j in range(1, C)
+        for j in far_first(C)
     ]
 
     for copy in zb_copies:
@@ -271,7 +274,7 @@
         ybf[r, :JJ, :] = total[r * JJ:(r + 1) * JJ]
     yb_copies = [
         send(ybf.at[(rep + j) % R], ybrecv.at[j], yb_s.at[j], yb_r.at[j], {"rep": (rep + j) % R})
-        for j in range(1, R)
+        for j in far_first(R)
     ]
     for c, k in dp_peers:
         p_copies[c, k].wait_recv()
@@ -301,12 +304,13 @@
     full[dp, rep] = jnp.concatenate([total[:ZA], total_b[:JJ]], axis=0).astype(bf16)
     ay_copies = [
         send(full.at[dp, rep], full.at[dp, rep], ay_s.at[j], ay_r.at[j], {"rep": (rep + j) % R})
-        for j in range(1, R)
-    ]
+        for j in far_first(R)
+    ]
+    ay_at = dict(zip(far_first(R), ay_copies))
     ad_copies = []
     for j in [0] + sorted(range(1, R), key=lambda j: min(j, R - j)):
         if j:
-            ay_copies[j - 1].wait_recv()
+            ay_at[j].wait_recv()
         piece = full.at[dp, (rep + R - j) % R]
         for c, k in dp_peers:
             ad_copies.append(

time: 80.2 us -> 79.1 us (0.986)
  Pallas kernels: 76.6 us -> 75.5 us
    pallas_call x1, Pallas kernels: 76.6 us -> 75.5 us  [local(): pl.pallas_call(body, out_shape=(jax.ShapeDtypeStruct((T, QW), bf16), jax....]
where the time goes in v6:
time: 79.1 us; the launch traced here: 78.8 us
  Pallas kernels  75.5 us (95%)
  local copies, waits for them, and re-layouts  2.74 us (3%)
    pallas_call x1, Pallas kernels, local(): pl.pallas_call(body, out_shape=(jax.ShapeDtypeStruct((T, QW), bf16), jax....  75.5 us
    unnamed x4, local copies, waits for them, and re-layouts  2.74 us

profile of v6, /device:TPU:1, one launch (start us, length us, event | category | flops | bytes accessed | tf_op | source)
XLA Modules:
  0.0 78.8 jit_solution(14869533628340991625)
XLA Ops:
  0.6 75.5 %shard_map.86 = (bf16[128,2048]{1,0:T(8,128)(2,1)}, f32[256,512]{1,0:T(8,128)}) custom-call(bf16[128,4096]{1,0:T(8,128)(2,1)} %bitcast.6, bf16[128,2048]{1,0:T(8,128)(2,1)} %bitcast.8, bf16[128,512]{1,0:T(8,128)(2,1)} %bitcast.10, bf16[128,512]{1,0:T(8,128)(2,1)} %bitcast.11, bf16[128,2048]{1,0:T(8,128)(2,1)} %bitcast.9, s32[1,128]{1,0:T(1,128)} %refs_5_.1, ...), custom_call_target="tpu_custom_call" | custom-call | tf_op jit(solution)/shard_map/pallas_call | solution.py:354
  76.1 0.0 copy-start
  76.1 1.9 %copy.11 = bf16[1,128,2048]{2,1,0:T(8,128)(2,1)} copy(bf16[1,128,2048]{2,1,0:T(8,128)(2,1)} %bitcast.7) | data formatting | bytes 1048576
  78.1 0.0 copy-done
  78.1 0.8 %copy.12 = f32[256,512]{1,0:T(8,128)} copy(f32[256,512]{1,0:T(8,128)S(1)} %copy-done) | data formatting | bytes 1048576
Async XLA Ops:
  76.1 2.0 %copy-start = (f32[256,512]{1,0:T(8,128)S(1)}, f32[256,512]{1,0:T(8,128)}, u32[]{:S(2)}) copy-start(f32[256,512]{1,0:T(8,128)} %get-tuple-element.9) | copy-start | bytes 1572868
